TPU v7x, 256 devices: a whole 4x4x8 slice. The times are simulated.
256 devices in a mesh: row: 16 (over z_lo, y, core), col: 16 (over x, z_hi).
Axes of the slice: x: 4, y: 4, z: 8 (z_hi: 4, z_lo: 2; z = z_hi * 2 + z_lo), core: 2. Of those that a mesh axis runs over, the one named last changes fastest.
Arguments:
- positions: float32 [3, 262144], P(None, ('col', 'row')), may hold values from 0 to 16
- velocity: float32 [3, 262144], P(None, ('col', 'row')), may hold values from -6 to 6
- applied: float32 [3, 262144], P(None, ('col', 'row')), may hold values from -12 to 12
- suscept: float32 [262144], P(('col', 'row')), may hold values from 0.05 to 0.3
- contact_owner: int32 [16, 16, 16, 512], P('col', 'row'), may hold values from 0 to 1023
- contact_partner: int32 [16, 16, 16, 512], P('col', 'row'), may hold values from 0 to 1023
- contact_count: int32 [16, 16, 16], P('col', 'row'), may hold values from 1 to 512, as said below
Outputs:
- moments: float32 [3, 262144], P(None, ('col', 'row'))
- forces: float32 [3, 262144], P(None, ('col', 'row'))
Inputs may be any that keep to these rules, and one draw needn't show every extreme that they name: `contact_count`: in every draw one column receives full blocks of 512 live slots from every device; the other columns' blocks are filled to different depths.
All inputs are finite; a program needn't handle non-finite values.
Results may differ from a plain program's by a relative error of at most 0.0003.
Values sent between devices are 32-bit elements; how exact they have to be, the bound alone decides.
A program may use at most 64 MiB of HBM per device.

v0:
```python
import math
import jax
import jax.numpy as jnp
from jax import lax
from jax.sharding import PartitionSpec as P

ITERS = 2


def dipole_block(target_pos, target_ids, source_pos, source_mom, source_ids):
    offset = target_pos[:, :, None] - source_pos[:, None, :]
    radius_sq = jnp.sum(offset * offset, axis=0) + 1.0
    inverse_r = lax.rsqrt(radius_sq)
    inverse_cube = inverse_r * inverse_r * inverse_r
    inverse_fifth = inverse_cube * inverse_r * inverse_r
    keep_mask = target_ids[:, None] != source_ids[None, :]
    projection = jnp.sum(offset * source_mom[:, None, :], axis=0)
    radial_coef = jnp.where(keep_mask, 3.0 * projection * inverse_fifth, 0.0)
    direct_coef = jnp.where(keep_mask, inverse_cube, 0.0)
    return jnp.sum(radial_coef[None] * offset, axis=2) - jnp.sum(
        direct_coef[None] * source_mom[:, None, :], axis=2
    )


def local_field(target_pos, target_ids, source_pos, source_mom, source_ids):
    target_len = target_pos.shape[1]
    source_len = source_pos.shape[1]
    target_block = math.gcd(target_len, 128)
    source_block = math.gcd(source_len, 512)
    target_count = target_len // target_block
    source_count = source_len // source_block
    source_blocks = (
        source_pos.reshape(3, source_count, source_block).transpose(1, 0, 2),
        source_mom.reshape(3, source_count, source_block).transpose(1, 0, 2),
        source_ids.reshape(source_count, source_block),
    )
    target_blocks = (
        target_pos.reshape(3, target_count, target_block).transpose(1, 0, 2),
        target_ids.reshape(target_count, target_block),
    )

    def per_target(target_pair):

        def add_block(field_sum, source_triple):
            return (
                field_sum
                + dipole_block(
                    target_pair[0],
                    target_pair[1],
                    source_triple[0],
                    source_triple[1],
                    source_triple[2],
                ),
                None,
            )

        field_sum, unused = lax.scan(
            add_block, jnp.zeros((3, target_block), jnp.float32), source_blocks
        )
        return field_sum

    result_blocks = lax.map(per_target, target_blocks)
    return result_blocks.transpose(1, 0, 2).reshape(3, target_len)


def pair_force(one_side, other_side):
    separation = one_side[0:3] - other_side[0:3]
    distance = jnp.sqrt(jnp.sum(separation * separation, axis=0) + 1.0)
    normal = separation / distance
    mom_one = one_side[6:9]
    mom_other = other_side[6:9]
    along_one = jnp.sum(mom_one * normal, axis=0)
    along_other = jnp.sum(mom_other * normal, axis=0)
    mom_dot = jnp.sum(mom_one * mom_other, axis=0)
    magnetic = 3.0 * (
        along_one * mom_other
        + along_other * mom_one
        + (mom_dot - 5.0 * along_one * along_other) * normal
    )
    spring = -0.03 * (distance - 1.0) * normal
    rel_speed = jnp.sum((one_side[3:6] - other_side[3:6]) * normal, axis=0)
    damping = -0.5 * rel_speed * normal
    return magnetic + spring + damping


def accumulate(slot_values, slot_ids, particle_count):
    flat_ids = slot_ids.reshape(-1)
    flat_values = slot_values.reshape(3, -1)
    return jnp.zeros((3, particle_count), jnp.float32).at[:, flat_ids].add(flat_values)


def on_device(positions, velocity, applied, suscept, contact_owner, contact_partner, contact_count):
    particle_count = positions.shape[1]
    row_index = lax.axis_index("row")
    own_ids = row_index * particle_count + jnp.arange(particle_count, dtype=jnp.int32)
    moments = suscept[None, :] * applied
    for iteration in range(ITERS):
        shard_pieces = (
            lax.all_gather(positions, "row", axis=1, tiled=True),
            lax.all_gather(moments, "row", axis=1, tiled=True),
        )
        piece_len = shard_pieces[0].shape[1]
        source_ids = jnp.arange(piece_len, dtype=jnp.int32)
        field_sum = local_field(positions, own_ids, shard_pieces[0], shard_pieces[1], source_ids)
        moments = suscept[None, :] * (applied + field_sum)
    col_count = contact_owner.shape[2]
    slot_count = contact_owner.shape[3]
    owner_ids = contact_owner.reshape(col_count, slot_count)
    partner_ids = contact_partner.reshape(col_count, slot_count)
    count_here = contact_count.reshape(col_count)
    live_mask = (jnp.arange(slot_count, dtype=jnp.int32)[None, :] < count_here[:, None]).astype(
        jnp.float32
    )
    state_rows = jnp.concatenate([positions, velocity, moments], axis=0)
    owner_rows = jnp.take(state_rows, owner_ids, axis=1)
    asked_ids = lax.all_to_all(partner_ids, "col", split_axis=0, concat_axis=0, tiled=True)
    looked_up = jnp.take(state_rows, asked_ids, axis=1)
    sent_rows = lax.all_to_all(looked_up, "col", split_axis=1, concat_axis=1, tiled=True)
    partner_rows, asked_ids = (sent_rows, asked_ids[None])
    slot_force = pair_force(owner_rows, partner_rows) * live_mask[None]
    owner_force = accumulate(slot_force, owner_ids, particle_count)
    returned = lax.all_to_all(slot_force, "col", split_axis=1, concat_axis=1, tiled=True)
    forces = owner_force - accumulate(returned, asked_ids[0], particle_count)
    return (moments, forces)


def solution(mesh):
    placed = (
        P(None, ("col", "row")),
        P(None, ("col", "row")),
        P(None, ("col", "row")),
        P(("col", "row")),
        P("col", "row", None, None),
        P("col", "row", None, None),
        P("col", "row", None),
    )
    return jax.shard_map(
        on_device,
        mesh=mesh,
        in_specs=placed,
        out_specs=(P(None, ("col", "row")), P(None, ("col", "row"))),
        check_vma=False,
    )
```

profile of v0, /device:TPU:1, one launch (start us, length us, event | category | flops | bytes accessed | tf_op | source)
XLA Modules:
  0.0 661.3 jit_solution(5421907334864235557)
XLA Ops:
  0.6 1.4 all_to_all.14
  2.0 11.6 %all-to-all-start = ((s32[16,1,512]{2,1,0:T(1,128)}), s32[16,1,512]{2,1,0:T(1,128)S(1)}, u32[]{:S(2)}, u32[]{:S(2)}) async-start(s32[16,1,512]{2,1,0:T(1,128)} %all_to_all.14), calls=%async_computation | async-start | bytes 65536 | tf_op jit(solution)/shard_map/all_to_all | solution.py:116
  13.6 0.8 fusion.23
  14.4 0.8 copy.46
  15.2 21.1 %all_gather.10 = f32[3,16384]{1,0:T(4,128)S(1)} all-gather(f32[3,1024]{1,0:T(4,128)} %param.17), channel_id=1, replica_groups=mesh['row'=16,'col'=16] {'row'}, dimensions={1}, use_global_device_ids=true | all-gather | bytes 208896 | tf_op jit(solution)/shard_map/all_gather | solution.py:99
  36.3 0.7 broadcast_multiply_fusion.1
  37.0 17.0 %all_gather.11 = f32[3,16384]{1,0:T(4,128)S(1)} all-gather(f32[3,1024]{1,0:T(4,128)S(1)} %broadcast_multiply_fusion.1), channel_id=1, replica_groups=mesh['row'=16,'col'=16] {'row'}, dimensions={1}, use_global_device_ids=true | all-gather | bytes 208896 | tf_op jit(solution)/shard_map/all_gather | solution.py:100
  54.0 204.9 %while.47 = (s32[]{:T(128)}, f32[8,3,128]{2,1,0:T(4,128)S(1)}, f32[8,3,128]{2,1,0:T(4,128)}, s32[8,128]{1,0:T(8,128)S(1)}, f32[32,3,512]{2,1,0:T(4,128)S(1)}, /*...) while((s32[]{:T(128)}, f32[8,3,128]{2,1,0:T(4,128)S(1)}, ...), condition=%wide.region_7.8_spmd.clone, body=%wide.region_0.7_spmd.clone.sunk | while | flops 2523525 | bytes 2239280 | solution.py:62
  54.0 0.7 dynamic-slice_bitcast_fusion.10
  54.7 24.9 %while.50 = (s32[]{:T(128)}, f32[3,128]{1,0:T(4,128)S(1)}, s32[128]{0:T(128)S(1)}, s32[32,512]{1,0:T(8,128)S(1)}, f32[3,128]{1,0:T(4,128)S(1)}, /*index=5*/f32[3...) while((s32[]{:T(128)}, f32[3,128]{1,0:T(4,128)S(1)}, s32[128]{0:T(128)S(1)}, ...), condition=%wide.region_6.6_spmd.clone, body=%wide.region_1.5_spmd.clone.sunk | while | flops 2490755 | bytes 2165359 | solution.py:57
  80.3 24.9 %while.50 = (s32[]{:T(128)}, f32[3,128]{1,0:T(4,128)S(1)}, s32[128]{0:T(128)S(1)}, s32[32,512]{1,0:T(8,128)S(1)}, f32[3,128]{1,0:T(4,128)S(1)}, /*index=5*/f32[3...) while((s32[]{:T(128)}, f32[3,128]{1,0:T(4,128)S(1)}, s32[128]{0:T(128)S(1)}, ...), condition=%wide.region_6.6_spmd.clone, body=%wide.region_1.5_spmd.clone.sunk | while | flops 2490755 | bytes 2165359 | solution.py:57
  105.9 24.9 %while.50 = (s32[]{:T(128)}, f32[3,128]{1,0:T(4,128)S(1)}, s32[128]{0:T(128)S(1)}, s32[32,512]{1,0:T(8,128)S(1)}, f32[3,128]{1,0:T(4,128)S(1)}, /*index=5*/f32[3...) while((s32[]{:T(128)}, f32[3,128]{1,0:T(4,128)S(1)}, s32[128]{0:T(128)S(1)}, ...), condition=%wide.region_6.6_spmd.clone, body=%wide.region_1.5_spmd.clone.sunk | while | flops 2490755 | bytes 2165359 | solution.py:57
  131.5 24.9 %while.50 = (s32[]{:T(128)}, f32[3,128]{1,0:T(4,128)S(1)}, s32[128]{0:T(128)S(1)}, s32[32,512]{1,0:T(8,128)S(1)}, f32[3,128]{1,0:T(4,128)S(1)}, /*index=5*/f32[3...) while((s32[]{:T(128)}, f32[3,128]{1,0:T(4,128)S(1)}, s32[128]{0:T(128)S(1)}, ...), condition=%wide.region_6.6_spmd.clone, body=%wide.region_1.5_spmd.clone.sunk | while | flops 2490755 | bytes 2165359 | solution.py:57
  157.2 24.9 %while.50 = (s32[]{:T(128)}, f32[3,128]{1,0:T(4,128)S(1)}, s32[128]{0:T(128)S(1)}, s32[32,512]{1,0:T(8,128)S(1)}, f32[3,128]{1,0:T(4,128)S(1)}, /*index=5*/f32[3...) while((s32[]{:T(128)}, f32[3,128]{1,0:T(4,128)S(1)}, s32[128]{0:T(128)S(1)}, ...), condition=%wide.region_6.6_spmd.clone, body=%wide.region_1.5_spmd.clone.sunk | while | flops 2490755 | bytes 2165359 | solution.py:57
  182.8 24.9 %while.50 = (s32[]{:T(128)}, f32[3,128]{1,0:T(4,128)S(1)}, s32[128]{0:T(128)S(1)}, s32[32,512]{1,0:T(8,128)S(1)}, f32[3,128]{1,0:T(4,128)S(1)}, /*index=5*/f32[3...) while((s32[]{:T(128)}, f32[3,128]{1,0:T(4,128)S(1)}, s32[128]{0:T(128)S(1)}, ...), condition=%wide.region_6.6_spmd.clone, body=%wide.region_1.5_spmd.clone.sunk | while | flops 2490755 | bytes 2165359 | solution.py:57
  208.4 24.9 %while.50 = (s32[]{:T(128)}, f32[3,128]{1,0:T(4,128)S(1)}, s32[128]{0:T(128)S(1)}, s32[32,512]{1,0:T(8,128)S(1)}, f32[3,128]{1,0:T(4,128)S(1)}, /*index=5*/f32[3...) while((s32[]{:T(128)}, f32[3,128]{1,0:T(4,128)S(1)}, s32[128]{0:T(128)S(1)}, ...), condition=%wide.region_6.6_spmd.clone, body=%wide.region_1.5_spmd.clone.sunk | while | flops 2490755 | bytes 2165359 | solution.py:57
  234.0 24.9 %while.50 = (s32[]{:T(128)}, f32[3,128]{1,0:T(4,128)S(1)}, s32[128]{0:T(128)S(1)}, s32[32,512]{1,0:T(8,128)S(1)}, f32[3,128]{1,0:T(4,128)S(1)}, /*index=5*/f32[3...) while((s32[]{:T(128)}, f32[3,128]{1,0:T(4,128)S(1)}, s32[128]{0:T(128)S(1)}, ...), condition=%wide.region_6.6_spmd.clone, body=%wide.region_1.5_spmd.clone.sunk | while | flops 2490755 | bytes 2165359 | solution.py:57
  258.9 18.3 %all_gather.12 = f32[3,16384]{1,0:T(4,128)S(1)} all-gather(f32[3,1024]{1,0:T(4,128)S(1)} %fusion.26), channel_id=1, replica_groups=mesh['row'=16,'col'=16] {'row'}, dimensions={1}, use_global_device_ids=true | all-gather | bytes 208896 | tf_op jit(solution)/shard_map/all_gather | solution.py:100
  277.2 204.9 %while.49 = (s32[]{:T(128)}, f32[8,3,128]{2,1,0:T(4,128)S(1)}, f32[8,3,128]{2,1,0:T(4,128)}, s32[8,128]{1,0:T(8,128)S(1)}, f32[32,3,512]{2,1,0:T(4,128)S(1)}, /*...) while((s32[]{:T(128)}, f32[8,3,128]{2,1,0:T(4,128)S(1)}, ...), condition=%wide.region_15.16_spmd.clone, body=%wide.region_8.15_spmd.clone.sunk | while | flops 2523525 | bytes 2239280 | solution.py:62
  277.2 0.7 dynamic-slice_bitcast_fusion.11
  278.0 24.9 %while.51 = (s32[]{:T(128)}, f32[3,128]{1,0:T(4,128)S(1)}, s32[128]{0:T(128)S(1)}, s32[32,512]{1,0:T(8,128)S(1)}, f32[3,128]{1,0:T(4,128)S(1)}, /*index=5*/f32[3...) while((s32[]{:T(128)}, f32[3,128]{1,0:T(4,128)S(1)}, s32[128]{0:T(128)S(1)}, ...), condition=%wide.region_14.14_spmd.clone, body=%wide.region_9.13_spmd.clone.sunk | while | flops 2490755 | bytes 2165359 | solution.py:57
  302.9 0.7 dynamic-slice_bitcast_fusion.11
  303.6 24.9 %while.51 = (s32[]{:T(128)}, f32[3,128]{1,0:T(4,128)S(1)}, s32[128]{0:T(128)S(1)}, s32[32,512]{1,0:T(8,128)S(1)}, f32[3,128]{1,0:T(4,128)S(1)}, /*index=5*/f32[3...) while((s32[]{:T(128)}, f32[3,128]{1,0:T(4,128)S(1)}, s32[128]{0:T(128)S(1)}, ...), condition=%wide.region_14.14_spmd.clone, body=%wide.region_9.13_spmd.clone.sunk | while | flops 2490755 | bytes 2165359 | solution.py:57
  328.5 0.7 dynamic-slice_bitcast_fusion.11
  329.2 24.9 %while.51 = (s32[]{:T(128)}, f32[3,128]{1,0:T(4,128)S(1)}, s32[128]{0:T(128)S(1)}, s32[32,512]{1,0:T(8,128)S(1)}, f32[3,128]{1,0:T(4,128)S(1)}, /*index=5*/f32[3...) while((s32[]{:T(128)}, f32[3,128]{1,0:T(4,128)S(1)}, s32[128]{0:T(128)S(1)}, ...), condition=%wide.region_14.14_spmd.clone, body=%wide.region_9.13_spmd.clone.sunk | while | flops 2490755 | bytes 2165359 | solution.py:57
  354.1 0.7 dynamic-slice_bitcast_fusion.11
  354.8 24.9 %while.51 = (s32[]{:T(128)}, f32[3,128]{1,0:T(4,128)S(1)}, s32[128]{0:T(128)S(1)}, s32[32,512]{1,0:T(8,128)S(1)}, f32[3,128]{1,0:T(4,128)S(1)}, /*index=5*/f32[3...) while((s32[]{:T(128)}, f32[3,128]{1,0:T(4,128)S(1)}, s32[128]{0:T(128)S(1)}, ...), condition=%wide.region_14.14_spmd.clone, body=%wide.region_9.13_spmd.clone.sunk | while | flops 2490755 | bytes 2165359 | solution.py:57
  379.7 0.7 dynamic-slice_bitcast_fusion.11
  380.4 24.9 %while.51 = (s32[]{:T(128)}, f32[3,128]{1,0:T(4,128)S(1)}, s32[128]{0:T(128)S(1)}, s32[32,512]{1,0:T(8,128)S(1)}, f32[3,128]{1,0:T(4,128)S(1)}, /*index=5*/f32[3...) while((s32[]{:T(128)}, f32[3,128]{1,0:T(4,128)S(1)}, s32[128]{0:T(128)S(1)}, ...), condition=%wide.region_14.14_spmd.clone, body=%wide.region_9.13_spmd.clone.sunk | while | flops 2490755 | bytes 2165359 | solution.py:57
  405.3 0.7 dynamic-slice_bitcast_fusion.11
  406.0 24.9 %while.51 = (s32[]{:T(128)}, f32[3,128]{1,0:T(4,128)S(1)}, s32[128]{0:T(128)S(1)}, s32[32,512]{1,0:T(8,128)S(1)}, f32[3,128]{1,0:T(4,128)S(1)}, /*index=5*/f32[3...) while((s32[]{:T(128)}, f32[3,128]{1,0:T(4,128)S(1)}, s32[128]{0:T(128)S(1)}, ...), condition=%wide.region_14.14_spmd.clone, body=%wide.region_9.13_spmd.clone.sunk | while | flops 2490755 | bytes 2165359 | solution.py:57
  430.9 0.7 dynamic-slice_bitcast_fusion.11
  431.6 24.9 %while.51 = (s32[]{:T(128)}, f32[3,128]{1,0:T(4,128)S(1)}, s32[128]{0:T(128)S(1)}, s32[32,512]{1,0:T(8,128)S(1)}, f32[3,128]{1,0:T(4,128)S(1)}, /*index=5*/f32[3...) while((s32[]{:T(128)}, f32[3,128]{1,0:T(4,128)S(1)}, s32[128]{0:T(128)S(1)}, ...), condition=%wide.region_14.14_spmd.clone, body=%wide.region_9.13_spmd.clone.sunk | while | flops 2490755 | bytes 2165359 | solution.py:57
  457.2 24.9 %while.51 = (s32[]{:T(128)}, f32[3,128]{1,0:T(4,128)S(1)}, s32[128]{0:T(128)S(1)}, s32[32,512]{1,0:T(8,128)S(1)}, f32[3,128]{1,0:T(4,128)S(1)}, /*index=5*/f32[3...) while((s32[]{:T(128)}, f32[3,128]{1,0:T(4,128)S(1)}, s32[128]{0:T(128)S(1)}, ...), condition=%wide.region_14.14_spmd.clone, body=%wide.region_9.13_spmd.clone.sunk | while | flops 2490755 | bytes 2165359 | solution.py:57
  482.2 0.7 pad_maximum_fusion
  483.3 27.7 %gather_fusion.1 = f32[8192,9]{1,0:T(8,128)} fusion(f32[9,1024]{0,1:T(8,128)S(1)} %copy.38, s32[8192]{0:T(1024)S(1)} %broadcast_clamp_fusion), kind=kCustom, calls=%fused_computation.1.clone | custom fusion | bytes 622592 | tf_op jit(solution)/shard_map/jit(_take)/gather | solution.py:117
  511.0 2.8 copy.41
  513.9 0.9 select_bitcast_fusion
  514.7 9.5 %all-to-all-start.1 = ((f32[9,16,512]{2,0,1:T(8,128)}), f32[9,16,512]{2,0,1:T(8,128)S(1)}, u32[]{:S(2)}, u32[]{:S(2)}) async-start(f32[9,16,512]{2,0,1:T(8,128)} %select_bitcast_fusion), calls=%async_computation.1 | async-start | bytes 1048576 | tf_op jit(solution)/shard_map/all_to_all | solution.py:118
  524.3 27.7 %gather_fusion = f32[8192,9]{1,0:T(8,128)} fusion(f32[9,1024]{0,1:T(8,128)S(1)} %copy.38, s32[8192]{0:T(1024)S(1)} %broadcast_clamp_fusion.1), kind=kCustom, calls=%fused_computation.clone | custom fusion | bytes 622592 | tf_op jit(solution)/shard_map/jit(_take)/gather | solution.py:115
  552.0 2.8 copy.39
  555.6 0.9 add_multiply_fusion
  556.4 9.1 %all-to-all-start.2 = ((f32[3,16,512]{2,0,1:T(4,128)}), f32[3,16,512]{2,0,1:T(4,128)S(1)}, u32[]{:S(2)}, u32[]{:S(2)}) async-start(f32[3,16,512]{2,0,1:T(4,128)} %add_multiply_fusion), calls=%async_computation.2 | async-start | bytes 262144 | tf_op jit(solution)/shard_map/all_to_all | solution.py:122
  565.5 3.4 copy.42
  569.0 44.4 %scatter_custom_fusion = f32[3,1024]{0,1:T(8,128)S(1)} fusion(s32[8192]{0:T(1024)S(1)} %bitcast.120, f32[8192,3]{1,0:T(8,128)} %copy.42, f32[]{:T(128)} %constant.84.clone.1), kind=kCustom, calls=%fused_computation.54 | custom fusion | flops 24576 | bytes 12800 | tf_op jit(solution)/shard_map/scatter-add | solution.py:89
  613.4 2.6 copy.43
  616.0 44.4 %scatter_custom_fusion.1 = f32[3,1024]{0,1:T(8,128)S(1)} fusion(s32[8192]{0:T(1024)S(1)} %bitcast.121, f32[8192,3]{1,0:T(8,128)} %copy.43, f32[]{:T(128)} %constant.84.clone.1), kind=kCustom, calls=%fused_computation.52 | custom fusion | flops 24576 | bytes 12800 | tf_op jit(solution)/shard_map/scatter-add | solution.py:89
  660.5 0.8 copy.44
  (3693 shorter events, 380.1 us)
Async XLA Ops:
  2.0 481.2 %all-to-all-start = ((s32[16,1,512]{2,1,0:T(1,128)}), s32[16,1,512]{2,1,0:T(1,128)S(1)}, u32[]{:S(2)}, u32[]{:S(2)}) async-start(s32[16,1,512]{2,1,0:T(1,128)} %all_to_all.14), calls=%async_computation | async-start | bytes 65536 | tf_op jit(solution)/shard_map/all_to_all | solution.py:116
  54.0 204.9 %copy-start.1 = (f32[3,1024]{1,0:T(4,128)S(1)}, f32[3,1024]{1,0:T(4,128)}, u32[]{:S(2)}) copy-start(f32[3,1024]{1,0:T(4,128)} %param.19) | copy-start | bytes 36868
  54.0 204.9 %copy-start.3 = (f32[1024]{0:T(1024)S(1)}, f32[1024]{0:T(1024)}, u32[]{:S(2)}) copy-start(f32[1024]{0:T(1024)} %param.20) | copy-start | bytes 12292
  277.2 205.0 %copy-start.4 = (f32[3,1024]{1,0:T(4,128)S(1)}, f32[3,1024]{1,0:T(4,128)}, u32[]{:S(2)}) copy-start(f32[3,1024]{1,0:T(4,128)} %param.18) | copy-start | bytes 36868
  482.1 31.7 %copy-start.2 = (f32[3,1024]{1,0:T(4,128)}, f32[3,1024]{1,0:T(4,128)S(1)}, u32[]{:S(2)}) copy-start(f32[3,1024]{1,0:T(4,128)S(1)} %fusion.25) | copy-start | bytes 36868
  483.3 40.9 %copy-start.5 = (s32[1,1,16]{2,1,0:T(1,128)S(1)}, s32[1,1,16]{2,1,0:T(1,128)}, u32[]{:S(2)}) copy-start(s32[1,1,16]{2,1,0:T(1,128)} %param.23) | copy-start | bytes 196
  514.7 40.1 %copy-start = (s32[1,1,16,512]{3,2,1,0:T(8,128)S(1)}, s32[1,1,16,512]{3,2,1,0:T(8,128)}, u32[]{:S(2)}) copy-start(s32[1,1,16,512]{3,2,1,0:T(8,128)} %param.21) | copy-start | bytes 98308
  514.7 40.2 %all-to-all-start.1 = ((f32[9,16,512]{2,0,1:T(8,128)}), f32[9,16,512]{2,0,1:T(8,128)S(1)}, u32[]{:S(2)}, u32[]{:S(2)}) async-start(f32[9,16,512]{2,0,1:T(8,128)} %select_bitcast_fusion), calls=%async_computation.1 | async-start | bytes 1048576 | tf_op jit(solution)/shard_map/all_to_all | solution.py:118
  556.4 57.0 %all-to-all-start.2 = ((f32[3,16,512]{2,0,1:T(4,128)}), f32[3,16,512]{2,0,1:T(4,128)S(1)}, u32[]{:S(2)}, u32[]{:S(2)}) async-start(f32[3,16,512]{2,0,1:T(4,128)} %add_multiply_fusion), calls=%async_computation.2 | async-start | bytes 262144 | tf_op jit(solution)/shard_map/all_to_all | solution.py:122
where the time goes:
time: 663 us; the launch traced here: 661 us
  other arithmetic  455 us (69%)
  local copies, waits for them, and re-layouts  93.3 us (14%)
  blocking collectives  56.4 us (9%)
  starting transfers between devices  30.1 us (5%)
  loops' own time  25.3 us (4%)
    reduce_sum x512, other arithmetic, dipole_block(): jnp.sum(radial_coef[None] * offset, axis=2)  126 us
    reduce_sum x512, other arithmetic, dipole_block(): radius_sq = jnp.sum(offset * offset, axis=0) + 1.0  97 us
    scatter-add x2, other arithmetic, accumulate(): jnp.zeros((3, particle_count), jnp.float32).at[:, flat_ids].add(flat_values)  88.9 us
    reduce_sum x512, other arithmetic, dipole_block(): jnp.sum(direct_coef[None] * source_mom[:, None, :], axis=2)  76.8 us
    select_n x512, other arithmetic, dipole_block(): direct_coef = jnp.where(keep_mask, inverse_cube, 0.0)  54.2 us
    all_gather x2, blocking collectives, on_device(): lax.all_gather(moments, 'row', axis=1, tiled=True)  35.3 us
    gather x2, local copies, waits for them, and re-layouts, on_device(): looked_up = jnp.take(state_rows, asked_ids, axis=1)  30.5 us
    gather x2, local copies, waits for them, and re-layouts, on_device(): owner_rows = jnp.take(state_rows, owner_ids, axis=1)  30.5 us
  transfers between devices with their start and end apart: 3, of which 0 were waited for; matrix products, arithmetic and copies ran while one was open for 71% of the time, Pallas kernels for 0%

commit v1 on v0

--- a/solution.py
+++ b/solution.py
@@ -97,7 +97,7 @@
     for iteration in range(ITERS):
         shard_pieces = (
             lax.all_gather(positions, "row", axis=1, tiled=True),
-            lax.all_gather(moments, "row", axis=1, tiled=True),
+            jnp.concatenate(lax.all_gather(moments, "row"), axis=1),
         )
         piece_len = shard_pieces[0].shape[1]
         source_ids = jnp.arange(piece_len, dtype=jnp.int32)

time: 663 us -> 663 us (level)
  no operation moved by 1% of the time
where the time goes in v1:
time: 663 us; the launch traced here: 661 us
  other arithmetic  455 us (69%)
  local copies, waits for them, and re-layouts  93.3 us (14%)
  blocking collectives  56.4 us (9%)
  starting transfers between devices  30.1 us (5%)
  loops' own time  25.3 us (4%)
    reduce_sum x512, other arithmetic, dipole_block(): jnp.sum(radial_coef[None] * offset, axis=2)  126 us
    reduce_sum x512, other arithmetic, dipole_block(): radius_sq = jnp.sum(offset * offset, axis=0) + 1.0  97 us
    scatter-add x2, other arithmetic, accumulate(): jnp.zeros((3, particle_count), jnp.float32).at[:, flat_ids].add(flat_values)  88.9 us
    reduce_sum x512, other arithmetic, dipole_block(): jnp.sum(direct_coef[None] * source_mom[:, None, :], axis=2)  76.8 us
    select_n x512, other arithmetic, dipole_block(): direct_coef = jnp.where(keep_mask, inverse_cube, 0.0)  54.2 us
    all_gather x2, blocking collectives, on_device(): lax.all_gather(moments, 'row')  35.3 us
    gather x2, local copies, waits for them, and re-layouts, on_device(): looked_up = jnp.take(state_rows, asked_ids, axis=1)  30.5 us
    gather x2, local copies, waits for them, and re-layouts, on_device(): owner_rows = jnp.take(state_rows, owner_ids, axis=1)  30.5 us
  transfers between devices with their start and end apart: 3, of which 0 were waited for; matrix products, arithmetic and copies ran while one was open for 71% of the time, Pallas kernels for 0%

profile of v1, /device:TPU:1, one launch (start us, length us, event | category | flops | bytes accessed | tf_op | source)
XLA Modules:
  0.0 661.3 jit_solution(4805045142621232272)
XLA Ops:
  0.6 1.4 all_to_all.14
  2.0 11.6 %all-to-all-start = ((s32[16,1,512]{2,1,0:T(1,128)}), s32[16,1,512]{2,1,0:T(1,128)S(1)}, u32[]{:S(2)}, u32[]{:S(2)}) async-start(s32[16,1,512]{2,1,0:T(1,128)} %all_to_all.14), calls=%async_computation | async-start | bytes 65536 | tf_op jit(solution)/shard_map/all_to_all | solution.py:116
  13.6 0.8 fusion.23
  14.4 0.8 copy.40
  15.2 21.1 %all_gather.16 = f32[3,16384]{1,0:T(4,128)S(1)} all-gather(f32[3,1024]{1,0:T(4,128)} %param.17), channel_id=1, replica_groups=mesh['row'=16,'col'=16] {'row'}, dimensions={1}, use_global_device_ids=true | all-gather | bytes 208896 | tf_op jit(solution)/shard_map/all_gather | solution.py:99
  36.3 0.7 multiply_bitcast_fusion
  37.0 17.0 %all-gather.2 = f32[16,3,1024]{2,1,0:T(4,128)S(1)} all-gather(f32[1,3,1024]{2,1,0:T(4,128)S(1)} %multiply_bitcast_fusion), channel_id=2, replica_groups=mesh['row'=16,'col'=16] {'row'}, dimensions={0}, use_global_device_ids=true | all-gather | bytes 208896 | tf_op jit(solution)/shard_map/all_gather | solution.py:100
  54.0 204.9 %while.47 = (s32[]{:T(128)}, f32[8,3,128]{2,1,0:T(4,128)S(1)}, f32[8,3,128]{2,1,0:T(4,128)}, s32[8,128]{1,0:T(8,128)S(1)}, f32[32,3,512]{2,1,0:T(4,128)S(1)}, /*...) while((s32[]{:T(128)}, f32[8,3,128]{2,1,0:T(4,128)S(1)}, ...), condition=%wide.region_7.8_spmd.clone, body=%wide.region_0.7_spmd.clone.sunk | while | flops 2523525 | bytes 2239280 | solution.py:62
  54.0 0.7 dynamic-slice_bitcast_fusion.10
  54.7 24.9 %while.50 = (s32[]{:T(128)}, f32[3,128]{1,0:T(4,128)S(1)}, s32[128]{0:T(128)S(1)}, s32[32,512]{1,0:T(8,128)S(1)}, f32[3,128]{1,0:T(4,128)S(1)}, /*index=5*/f32[3...) while((s32[]{:T(128)}, f32[3,128]{1,0:T(4,128)S(1)}, s32[128]{0:T(128)S(1)}, ...), condition=%wide.region_6.6_spmd.clone, body=%wide.region_1.5_spmd.clone.sunk | while | flops 2490755 | bytes 2165359 | solution.py:57
  80.3 24.9 %while.50 = (s32[]{:T(128)}, f32[3,128]{1,0:T(4,128)S(1)}, s32[128]{0:T(128)S(1)}, s32[32,512]{1,0:T(8,128)S(1)}, f32[3,128]{1,0:T(4,128)S(1)}, /*index=5*/f32[3...) while((s32[]{:T(128)}, f32[3,128]{1,0:T(4,128)S(1)}, s32[128]{0:T(128)S(1)}, ...), condition=%wide.region_6.6_spmd.clone, body=%wide.region_1.5_spmd.clone.sunk | while | flops 2490755 | bytes 2165359 | solution.py:57
  105.9 24.9 %while.50 = (s32[]{:T(128)}, f32[3,128]{1,0:T(4,128)S(1)}, s32[128]{0:T(128)S(1)}, s32[32,512]{1,0:T(8,128)S(1)}, f32[3,128]{1,0:T(4,128)S(1)}, /*index=5*/f32[3...) while((s32[]{:T(128)}, f32[3,128]{1,0:T(4,128)S(1)}, s32[128]{0:T(128)S(1)}, ...), condition=%wide.region_6.6_spmd.clone, body=%wide.region_1.5_spmd.clone.sunk | while | flops 2490755 | bytes 2165359 | solution.py:57
  131.5 24.9 %while.50 = (s32[]{:T(128)}, f32[3,128]{1,0:T(4,128)S(1)}, s32[128]{0:T(128)S(1)}, s32[32,512]{1,0:T(8,128)S(1)}, f32[3,128]{1,0:T(4,128)S(1)}, /*index=5*/f32[3...) while((s32[]{:T(128)}, f32[3,128]{1,0:T(4,128)S(1)}, s32[128]{0:T(128)S(1)}, ...), condition=%wide.region_6.6_spmd.clone, body=%wide.region_1.5_spmd.clone.sunk | while | flops 2490755 | bytes 2165359 | solution.py:57
  157.2 24.9 %while.50 = (s32[]{:T(128)}, f32[3,128]{1,0:T(4,128)S(1)}, s32[128]{0:T(128)S(1)}, s32[32,512]{1,0:T(8,128)S(1)}, f32[3,128]{1,0:T(4,128)S(1)}, /*index=5*/f32[3...) while((s32[]{:T(128)}, f32[3,128]{1,0:T(4,128)S(1)}, s32[128]{0:T(128)S(1)}, ...), condition=%wide.region_6.6_spmd.clone, body=%wide.region_1.5_spmd.clone.sunk | while | flops 2490755 | bytes 2165359 | solution.py:57
  182.8 24.9 %while.50 = (s32[]{:T(128)}, f32[3,128]{1,0:T(4,128)S(1)}, s32[128]{0:T(128)S(1)}, s32[32,512]{1,0:T(8,128)S(1)}, f32[3,128]{1,0:T(4,128)S(1)}, /*index=5*/f32[3...) while((s32[]{:T(128)}, f32[3,128]{1,0:T(4,128)S(1)}, s32[128]{0:T(128)S(1)}, ...), condition=%wide.region_6.6_spmd.clone, body=%wide.region_1.5_spmd.clone.sunk | while | flops 2490755 | bytes 2165359 | solution.py:57
  208.4 24.9 %while.50 = (s32[]{:T(128)}, f32[3,128]{1,0:T(4,128)S(1)}, s32[128]{0:T(128)S(1)}, s32[32,512]{1,0:T(8,128)S(1)}, f32[3,128]{1,0:T(4,128)S(1)}, /*index=5*/f32[3...) while((s32[]{:T(128)}, f32[3,128]{1,0:T(4,128)S(1)}, s32[128]{0:T(128)S(1)}, ...), condition=%wide.region_6.6_spmd.clone, body=%wide.region_1.5_spmd.clone.sunk | while | flops 2490755 | bytes 2165359 | solution.py:57
  234.0 24.9 %while.50 = (s32[]{:T(128)}, f32[3,128]{1,0:T(4,128)S(1)}, s32[128]{0:T(128)S(1)}, s32[32,512]{1,0:T(8,128)S(1)}, f32[3,128]{1,0:T(4,128)S(1)}, /*index=5*/f32[3...) while((s32[]{:T(128)}, f32[3,128]{1,0:T(4,128)S(1)}, s32[128]{0:T(128)S(1)}, ...), condition=%wide.region_6.6_spmd.clone, body=%wide.region_1.5_spmd.clone.sunk | while | flops 2490755 | bytes 2165359 | solution.py:57
  258.9 18.3 %all-gather.3 = f32[16,3,1024]{2,1,0:T(4,128)S(1)} all-gather(f32[1,3,1024]{2,1,0:T(4,128)S(1)} %fusion.27), channel_id=3, replica_groups=mesh['row'=16,'col'=16] {'row'}, dimensions={0}, use_global_device_ids=true | all-gather | bytes 208896 | tf_op jit(solution)/shard_map/all_gather | solution.py:100
  277.2 204.9 %while.49 = (s32[]{:T(128)}, f32[8,3,128]{2,1,0:T(4,128)S(1)}, f32[8,3,128]{2,1,0:T(4,128)}, s32[8,128]{1,0:T(8,128)S(1)}, f32[32,3,512]{2,1,0:T(4,128)S(1)}, /*...) while((s32[]{:T(128)}, f32[8,3,128]{2,1,0:T(4,128)S(1)}, ...), condition=%wide.region_15.16_spmd.clone, body=%wide.region_8.15_spmd.clone.sunk | while | flops 2523525 | bytes 2239280 | solution.py:62
  277.2 0.7 dynamic-slice_bitcast_fusion.11
  278.0 24.9 %while.51 = (s32[]{:T(128)}, f32[3,128]{1,0:T(4,128)S(1)}, s32[128]{0:T(128)S(1)}, s32[32,512]{1,0:T(8,128)S(1)}, f32[3,128]{1,0:T(4,128)S(1)}, /*index=5*/f32[3...) while((s32[]{:T(128)}, f32[3,128]{1,0:T(4,128)S(1)}, s32[128]{0:T(128)S(1)}, ...), condition=%wide.region_14.14_spmd.clone, body=%wide.region_9.13_spmd.clone.sunk | while | flops 2490755 | bytes 2165359 | solution.py:57
  302.9 0.7 dynamic-slice_bitcast_fusion.11
  303.6 24.9 %while.51 = (s32[]{:T(128)}, f32[3,128]{1,0:T(4,128)S(1)}, s32[128]{0:T(128)S(1)}, s32[32,512]{1,0:T(8,128)S(1)}, f32[3,128]{1,0:T(4,128)S(1)}, /*index=5*/f32[3...) while((s32[]{:T(128)}, f32[3,128]{1,0:T(4,128)S(1)}, s32[128]{0:T(128)S(1)}, ...), condition=%wide.region_14.14_spmd.clone, body=%wide.region_9.13_spmd.clone.sunk | while | flops 2490755 | bytes 2165359 | solution.py:57
  328.5 0.7 dynamic-slice_bitcast_fusion.11
  329.2 24.9 %while.51 = (s32[]{:T(128)}, f32[3,128]{1,0:T(4,128)S(1)}, s32[128]{0:T(128)S(1)}, s32[32,512]{1,0:T(8,128)S(1)}, f32[3,128]{1,0:T(4,128)S(1)}, /*index=5*/f32[3...) while((s32[]{:T(128)}, f32[3,128]{1,0:T(4,128)S(1)}, s32[128]{0:T(128)S(1)}, ...), condition=%wide.region_14.14_spmd.clone, body=%wide.region_9.13_spmd.clone.sunk | while | flops 2490755 | bytes 2165359 | solution.py:57
  354.1 0.7 dynamic-slice_bitcast_fusion.11
  354.8 24.9 %while.51 = (s32[]{:T(128)}, f32[3,128]{1,0:T(4,128)S(1)}, s32[128]{0:T(128)S(1)}, s32[32,512]{1,0:T(8,128)S(1)}, f32[3,128]{1,0:T(4,128)S(1)}, /*index=5*/f32[3...) while((s32[]{:T(128)}, f32[3,128]{1,0:T(4,128)S(1)}, s32[128]{0:T(128)S(1)}, ...), condition=%wide.region_14.14_spmd.clone, body=%wide.region_9.13_spmd.clone.sunk | while | flops 2490755 | bytes 2165359 | solution.py:57
  379.7 0.7 dynamic-slice_bitcast_fusion.11
  380.4 24.9 %while.51 = (s32[]{:T(128)}, f32[3,128]{1,0:T(4,128)S(1)}, s32[128]{0:T(128)S(1)}, s32[32,512]{1,0:T(8,128)S(1)}, f32[3,128]{1,0:T(4,128)S(1)}, /*index=5*/f32[3...) while((s32[]{:T(128)}, f32[3,128]{1,0:T(4,128)S(1)}, s32[128]{0:T(128)S(1)}, ...), condition=%wide.region_14.14_spmd.clone, body=%wide.region_9.13_spmd.clone.sunk | while | flops 2490755 | bytes 2165359 | solution.py:57
  405.3 0.7 dynamic-slice_bitcast_fusion.11
  406.0 24.9 %while.51 = (s32[]{:T(128)}, f32[3,128]{1,0:T(4,128)S(1)}, s32[128]{0:T(128)S(1)}, s32[32,512]{1,0:T(8,128)S(1)}, f32[3,128]{1,0:T(4,128)S(1)}, /*index=5*/f32[3...) while((s32[]{:T(128)}, f32[3,128]{1,0:T(4,128)S(1)}, s32[128]{0:T(128)S(1)}, ...), condition=%wide.region_14.14_spmd.clone, body=%wide.region_9.13_spmd.clone.sunk | while | flops 2490755 | bytes 2165359 | solution.py:57
  430.9 0.7 dynamic-slice_bitcast_fusion.11
  431.6 24.9 %while.51 = (s32[]{:T(128)}, f32[3,128]{1,0:T(4,128)S(1)}, s32[128]{0:T(128)S(1)}, s32[32,512]{1,0:T(8,128)S(1)}, f32[3,128]{1,0:T(4,128)S(1)}, /*index=5*/f32[3...) while((s32[]{:T(128)}, f32[3,128]{1,0:T(4,128)S(1)}, s32[128]{0:T(128)S(1)}, ...), condition=%wide.region_14.14_spmd.clone, body=%wide.region_9.13_spmd.clone.sunk | while | flops 2490755 | bytes 2165359 | solution.py:57
  457.2 24.9 %while.51 = (s32[]{:T(128)}, f32[3,128]{1,0:T(4,128)S(1)}, s32[128]{0:T(128)S(1)}, s32[32,512]{1,0:T(8,128)S(1)}, f32[3,128]{1,0:T(4,128)S(1)}, /*index=5*/f32[3...) while((s32[]{:T(128)}, f32[3,128]{1,0:T(4,128)S(1)}, s32[128]{0:T(128)S(1)}, ...), condition=%wide.region_14.14_spmd.clone, body=%wide.region_9.13_spmd.clone.sunk | while | flops 2490755 | bytes 2165359 | solution.py:57
  482.2 0.7 pad_maximum_fusion
  483.3 27.7 %gather_fusion.1 = f32[8192,9]{1,0:T(8,128)} fusion(f32[9,1024]{0,1:T(8,128)S(1)} %copy.32, s32[8192]{0:T(1024)S(1)} %broadcast_clamp_fusion), kind=kCustom, calls=%fused_computation.1.clone | custom fusion | bytes 622592 | tf_op jit(solution)/shard_map/jit(_take)/gather | solution.py:117
  511.0 2.8 copy.35
  513.9 0.9 select_bitcast_fusion
  514.7 9.5 %all-to-all-start.1 = ((f32[9,16,512]{2,0,1:T(8,128)}), f32[9,16,512]{2,0,1:T(8,128)S(1)}, u32[]{:S(2)}, u32[]{:S(2)}) async-start(f32[9,16,512]{2,0,1:T(8,128)} %select_bitcast_fusion), calls=%async_computation.1 | async-start | bytes 1048576 | tf_op jit(solution)/shard_map/all_to_all | solution.py:118
  524.3 27.7 %gather_fusion = f32[8192,9]{1,0:T(8,128)} fusion(f32[9,1024]{0,1:T(8,128)S(1)} %copy.32, s32[8192]{0:T(1024)S(1)} %broadcast_clamp_fusion.1), kind=kCustom, calls=%fused_computation.clone | custom fusion | bytes 622592 | tf_op jit(solution)/shard_map/jit(_take)/gather | solution.py:115
  552.0 2.8 copy.33
  555.6 0.9 add_multiply_fusion
  556.4 9.1 %all-to-all-start.2 = ((f32[3,16,512]{2,0,1:T(4,128)}), f32[3,16,512]{2,0,1:T(4,128)S(1)}, u32[]{:S(2)}, u32[]{:S(2)}) async-start(f32[3,16,512]{2,0,1:T(4,128)} %add_multiply_fusion), calls=%async_computation.2 | async-start | bytes 262144 | tf_op jit(solution)/shard_map/all_to_all | solution.py:122
  565.5 3.4 copy.36
  569.0 44.4 %scatter_custom_fusion = f32[3,1024]{0,1:T(8,128)S(1)} fusion(s32[8192]{0:T(1024)S(1)} %bitcast.130, f32[8192,3]{1,0:T(8,128)} %copy.36, f32[]{:T(128)} %constant.84.clone.1), kind=kCustom, calls=%fused_computation.54 | custom fusion | flops 24576 | bytes 12800 | tf_op jit(solution)/shard_map/scatter-add | solution.py:89
  613.4 2.6 copy.37
  616.0 44.4 %scatter_custom_fusion.1 = f32[3,1024]{0,1:T(8,128)S(1)} fusion(s32[8192]{0:T(1024)S(1)} %bitcast.131, f32[8192,3]{1,0:T(8,128)} %copy.37, f32[]{:T(128)} %constant.84.clone.1), kind=kCustom, calls=%fused_computation.52 | custom fusion | flops 24576 | bytes 12800 | tf_op jit(solution)/shard_map/scatter-add | solution.py:89
  660.5 0.8 copy.38
  (3693 shorter events, 380.1 us)
Async XLA Ops:
  2.0 481.2 %all-to-all-start = ((s32[16,1,512]{2,1,0:T(1,128)}), s32[16,1,512]{2,1,0:T(1,128)S(1)}, u32[]{:S(2)}, u32[]{:S(2)}) async-start(s32[16,1,512]{2,1,0:T(1,128)} %all_to_all.14), calls=%async_computation | async-start | bytes 65536 | tf_op jit(solution)/shard_map/all_to_all | solution.py:116
  54.0 204.9 %copy-start.1 = (f32[3,1024]{1,0:T(4,128)S(1)}, f32[3,1024]{1,0:T(4,128)}, u32[]{:S(2)}) copy-start(f32[3,1024]{1,0:T(4,128)} %param.19) | copy-start | bytes 36868
  54.0 204.9 %copy-start.3 = (f32[1024]{0:T(1024)S(1)}, f32[1024]{0:T(1024)}, u32[]{:S(2)}) copy-start(f32[1024]{0:T(1024)} %param.20) | copy-start | bytes 12292
  277.2 205.0 %copy-start.4 = (f32[3,1024]{1,0:T(4,128)S(1)}, f32[3,1024]{1,0:T(4,128)}, u32[]{:S(2)}) copy-start(f32[3,1024]{1,0:T(4,128)} %param.18) | copy-start | bytes 36868
  482.1 31.7 %copy-start.2 = (f32[3,1024]{1,0:T(4,128)}, f32[3,1024]{1,0:T(4,128)S(1)}, u32[]{:S(2)}) copy-start(f32[3,1024]{1,0:T(4,128)S(1)} %fusion.25) | copy-start | bytes 36868
  483.3 40.9 %copy-start.5 = (s32[1,1,16]{2,1,0:T(1,128)S(1)}, s32[1,1,16]{2,1,0:T(1,128)}, u32[]{:S(2)}) copy-start(s32[1,1,16]{2,1,0:T(1,128)} %param.23) | copy-start | bytes 196
  514.7 40.1 %copy-start = (s32[1,1,16,512]{3,2,1,0:T(8,128)S(1)}, s32[1,1,16,512]{3,2,1,0:T(8,128)}, u32[]{:S(2)}) copy-start(s32[1,1,16,512]{3,2,1,0:T(8,128)} %param.21) | copy-start | bytes 98308
  514.7 40.2 %all-to-all-start.1 = ((f32[9,16,512]{2,0,1:T(8,128)}), f32[9,16,512]{2,0,1:T(8,128)S(1)}, u32[]{:S(2)}, u32[]{:S(2)}) async-start(f32[9,16,512]{2,0,1:T(8,128)} %select_bitcast_fusion), calls=%async_computation.1 | async-start | bytes 1048576 | tf_op jit(solution)/shard_map/all_to_all | solution.py:118
  556.4 57.0 %all-to-all-start.2 = ((f32[3,16,512]{2,0,1:T(4,128)}), f32[3,16,512]{2,0,1:T(4,128)S(1)}, u32[]{:S(2)}, u32[]{:S(2)}) async-start(f32[3,16,512]{2,0,1:T(4,128)} %add_multiply_fusion), calls=%async_computation.2 | async-start | bytes 262144 | tf_op jit(solution)/shard_map/all_to_all | solution.py:122
